TPU v7x, 32 devices: a whole 2x2x4 slice. The times are simulated.
32 devices in a mesh: grp: 2 (over y), ctx: 4 (over z), head: 4 (over x, core).
Axes of the slice: x: 2, y: 2, z: 4, core: 2. Of those that a mesh axis runs over, the one named last changes fastest.
Arguments:
- queries: bfloat16 [1024, 8192], P(('grp', 'ctx'), 'head'), parts along dimension 0, may hold values from -5 to 5
- keys: bfloat16 [1024, 1024], P(('grp', 'ctx'), 'head'), parts along dimension 0, may hold values from -5 to 5
- values: bfloat16 [1024, 1024], P(('grp', 'ctx'), 'head'), parts along dimension 0, may hold values from -6 to 6
- d_out: bfloat16 [1024, 8192], P(('grp', 'ctx'), 'head'), parts along dimension 0, may hold values from -6 to 6
- span_order: int32 [4], replicated, may hold values from 0 to 3, each once
- pattern: int32 [4, 2], replicated, may hold values from 0 to 3, as said below
Outputs:
- d_queries: bfloat16 [1024, 8192], P(('grp', 'ctx'), 'head'), parts along dimension 0
- key_gradients: bfloat16 [1024, 1024], P(('grp', 'ctx'), 'head'), parts along dimension 0
- value_gradients: bfloat16 [1024, 1024], P(('grp', 'ctx'), 'head'), parts along dimension 0
There are 2 independent parts, one for each index of `grp`. A program takes and returns all parts, laid end to end along the dimension named above; an argument that names none is the same for every part. Nothing has to cross between parts.
Inputs may be any that keep to these rules, and one draw needn't show every extreme that they name: `span_order`: a permutation of the 4 block positions. `pattern`: each row names 2 distinct blocks, its own block first.
All inputs are finite; a program needn't handle non-finite values.
Results may differ from a plain program's by a relative error of at most 0.0075.
Values may be sent and summed in bfloat16 or wider, within the bound.
No kernel may reach another device: no remote copies, remote signals or barrier semaphores. Data moves between devices by JAX's collectives and lax.ppermute only.
A program may use at most 64 MiB of HBM per device.

v0:
```python
import math
import jax
import jax.numpy as jnp
from jax import lax
from jax.sharding import PartitionSpec as P

QUERY_HEADS = 64
KEY_VALUE_HEADS = 8
HEAD_SIZE = 128
BLOCK = 128
NEG = -1e30


def heads_first(dense_matrix, key_value_count):
    return dense_matrix.reshape(
        dense_matrix.shape[0], key_value_count, QUERY_HEADS // KEY_VALUE_HEADS, HEAD_SIZE
    ).transpose(1, 2, 0, 3)


def key_mask(start, count, local_pattern, query_pos, span_order):
    key_blocks = start // BLOCK + jnp.arange(count // BLOCK, dtype=jnp.int32)
    named = jnp.any(local_pattern[:, :, None] == key_blocks[None, None, :], axis=1)
    local_blocks = local_pattern.shape[0]
    named_rows = jnp.broadcast_to(
        named[:, None, :, None], (local_blocks, BLOCK, count // BLOCK, BLOCK)
    )
    named_rows = named_rows.reshape(local_blocks * BLOCK, count)
    key_order = lax.dynamic_slice_in_dim(span_order, start // BLOCK, count // BLOCK, 0)
    key_pos = (key_order[:, None] * BLOCK + jnp.arange(BLOCK, dtype=jnp.int32)[None, :]).reshape(
        count
    )
    return named_rows & (key_pos[None, :] <= query_pos[:, None])


def sweep(step, carry, key_piece, value_piece, start):
    count = key_piece.shape[0]
    width = BLOCK * math.gcd(count // BLOCK, max(1, 512 // BLOCK))
    turns = count // width
    if turns == 1:
        return step(carry, key_piece, value_piece, start)

    def advance(index, inner):
        offset = index * width
        key_part = lax.dynamic_slice_in_dim(key_piece, offset, width, 0)
        value_part = lax.dynamic_slice_in_dim(value_piece, offset, width, 0)
        return step(inner, key_part, value_part, start + offset)

    return lax.fori_loop(0, turns, advance, carry)


def on_device(queries, keys, values, d_out, span_order, pattern):
    rows = queries.shape[0]
    key_value_count = keys.shape[1] // HEAD_SIZE
    query_group = QUERY_HEADS // KEY_VALUE_HEADS
    blocks_here = rows // BLOCK
    scale = 1.0 / math.sqrt(HEAD_SIZE)
    first_block = lax.axis_index("ctx") * blocks_here
    local_pattern = lax.dynamic_slice_in_dim(pattern, first_block, blocks_here, 0)
    local_order = lax.dynamic_slice_in_dim(span_order, first_block, blocks_here, 0)
    query_pos = (
        local_order[:, None] * BLOCK + jnp.arange(BLOCK, dtype=jnp.int32)[None, :]
    ).reshape(rows)
    query_heads = heads_first(queries, key_value_count)
    grad_heads = heads_first(d_out, key_value_count)
    total_rows = rows * lax.axis_size("ctx")

    def scores_for(key_piece):
        key_heads = key_piece.reshape(key_piece.shape[0], key_value_count, HEAD_SIZE)
        return (
            jnp.einsum("kgtd,rkd->kgtr", query_heads, key_heads, preferred_element_type=jnp.float32)
            * scale
        )

    def forward_step(carry, key_piece, value_piece, start):
        allowed = key_mask(start, key_piece.shape[0], local_pattern, query_pos, span_order)

        def forward_update(state):
            running_max, total, weighted = state
            scores = scores_for(key_piece)
            new_max = jnp.maximum(running_max, jnp.max(jnp.where(allowed, scores, NEG), axis=-1))
            factor = jnp.exp(running_max - new_max)
            weights = jnp.where(allowed, jnp.exp(scores - new_max[..., None]), 0.0)
            value_heads = value_piece.reshape(
                value_piece.shape[0], key_value_count, HEAD_SIZE
            ).astype(jnp.float32)
            product = jnp.einsum(
                "kgtr,rkd->kgtd", weights, value_heads, precision=lax.Precision.HIGHEST
            )
            return (
                new_max,
                total * factor + jnp.sum(weights, axis=-1),
                weighted * factor[..., None] + product,
            )

        return lax.cond(jnp.any(allowed), forward_update, lambda state: state, carry)

    def make_backward(log_total, delta, anchor):

        def step(carry, key_piece, value_piece, start):
            count = key_piece.shape[0]
            allowed = key_mask(start, count, local_pattern, query_pos, span_order)

            def step_update(state):
                query_grad, key_grads = state
                key_heads = key_piece.reshape(count, key_value_count, HEAD_SIZE)
                value_heads = value_piece.reshape(count, key_value_count, HEAD_SIZE)
                scores = scores_for(key_piece)
                probs = jnp.where(allowed, jnp.exp(scores - log_total[..., None]), 0.0)
                grad_probs = jnp.einsum(
                    "kgtd,rkd->kgtr", grad_heads, value_heads, preferred_element_type=jnp.float32
                )
                grad_scores = (probs * (grad_probs - delta[..., None])).astype(jnp.bfloat16)
                query_grad = query_grad + jnp.einsum(
                    "kgtr,rkd->kgtd", grad_scores, key_heads, preferred_element_type=jnp.float32
                )
                key_part = (
                    jnp.einsum(
                        "kgtr,kgtd->rkd",
                        grad_scores,
                        query_heads,
                        preferred_element_type=jnp.float32,
                    )
                    * scale
                )
                value_part = jnp.einsum(
                    "kgtr,kgtd->rkd",
                    probs.astype(jnp.bfloat16),
                    grad_heads,
                    preferred_element_type=jnp.float32,
                )
                joined = jnp.stack(
                    (
                        key_part.reshape(count, key_value_count * HEAD_SIZE),
                        value_part.reshape(count, key_value_count * HEAD_SIZE),
                    ),
                    axis=1,
                )
                offset = start - anchor
                former = lax.dynamic_slice_in_dim(key_grads, offset, count, 0)
                key_grads = lax.dynamic_update_slice_in_dim(key_grads, former + joined, offset, 0)
                return (query_grad, key_grads)

            return lax.cond(jnp.any(allowed), step_update, lambda state: state, carry)

        return step

    start_state = (
        jnp.full((key_value_count, query_group, rows), NEG, jnp.float32),
        jnp.zeros((key_value_count, query_group, rows), jnp.float32),
        jnp.zeros((key_value_count, query_group, rows, HEAD_SIZE), jnp.float32),
    )
    query_zero = jnp.zeros((key_value_count, query_group, rows, HEAD_SIZE), jnp.float32)
    state = sweep(
        forward_step,
        start_state,
        lax.all_gather(keys, "ctx", axis=0, tiled=True),
        lax.all_gather(values, "ctx", axis=0, tiled=True),
        jnp.int32(0),
    )
    running_max, total, weighted = state
    attended = weighted / total[..., None]
    log_total = running_max + jnp.log(total)
    delta = jnp.sum(grad_heads * attended, axis=-1)
    log_total, delta = (log_total, delta)
    both_step = make_backward(log_total, delta, 0)
    grad_zero = jnp.zeros((total_rows, 2, key_value_count * HEAD_SIZE), jnp.float32)
    query_grad, key_grads = sweep(
        both_step,
        (query_zero, grad_zero),
        lax.all_gather(keys, "ctx", axis=0, tiled=True),
        lax.all_gather(values, "ctx", axis=0, tiled=True),
        jnp.int32(0),
    )
    summed = lax.psum_scatter(key_grads, "ctx", scatter_dimension=0, tiled=True)
    d_queries = (
        (query_grad * scale)
        .transpose(2, 0, 1, 3)
        .reshape(rows, key_value_count * query_group * HEAD_SIZE)
        .astype(jnp.bfloat16)
    )
    key_gradients = summed[:, 0, :].astype(jnp.bfloat16)
    value_gradients = summed[:, 1, :].astype(jnp.bfloat16)
    return (d_queries, key_gradients, value_gradients)


def solution(mesh):
    return jax.shard_map(
        on_device,
        mesh=mesh,
        in_specs=(
            P(("grp", "ctx"), "head"),
            P(("grp", "ctx"), "head"),
            P(("grp", "ctx"), "head"),
            P(("grp", "ctx"), "head"),
            P(),
            P(),
        ),
        out_specs=(P(("grp", "ctx"), "head"), P(("grp", "ctx"), "head"), P(("grp", "ctx"), "head")),
        check_vma=False,
    )
```

profile of v0, /device:TPU:0, one launch (start us, length us, event | category | flops | bytes accessed | tf_op | source)
XLA Modules:
  0.0 102.2 jit_solution(14186769745617313074)
XLA Ops:
  7.9 1.2 %dynamic_slice.12 = s32[1]{0:T(128)} dynamic-slice(s32[4]{0:T(128)} %param.14, s32[]{:T(128)S(6)} %select_n.23), dynamic_slice_sizes={1} | dynamic-slice | bytes 12 | tf_op jit(solution)/shard_map/dynamic_slice | solution.py:59
  10.2 0.8 and_reduce_fusion
  11.7 15.8 %all_gather.8 = bf16[512,256]{1,0:T(8,128)(2,1)S(1)} all-gather(bf16[128,256]{1,0:T(8,128)(2,1)} %param.11), channel_id=1, replica_groups=mesh['grp'=2,'ctx'=4,'head'=4] {'ctx'}, dimensions={0}, use_global_device_ids=true | all-gather | bytes 327680 | tf_op jit(solution)/shard_map/all_gather | solution.py:170
  27.5 14.8 %all_gather.9 = bf16[512,256]{1,0:T(8,128)(2,1)S(1)} all-gather(bf16[128,256]{1,0:T(8,128)(2,1)} %param.12), channel_id=1, replica_groups=mesh['grp'=2,'ctx'=4,'head'=4] {'ctx'}, dimensions={0}, use_global_device_ids=true | all-gather | bytes 327680 | tf_op jit(solution)/shard_map/all_gather | solution.py:171
  42.3 1.3 %copy.29 = bf16[128,2048]{0,1:T(8,128)(2,1)S(1)} copy(bf16[128,2048]{1,0:T(8,128)(2,1)} %param.10) | data formatting | bytes 1048576 | tf_op args[0]
  43.6 1.3 %copy.31 = bf16[128,2048]{0,1:T(8,128)(2,1)S(1)} copy(bf16[128,2048]{1,0:T(8,128)(2,1)} %param.13) | data formatting | bytes 1048576 | tf_op args[3]
  45.0 0.8 copy-done.1
  46.3 8.0 %conditional.2 = (f32[2,8,128]{2,1,0:T(8,128)}, f32[2,8,128]{2,1,0:T(8,128)S(1)}, f32[2,8,128,128]{3,2,1,0:T(8,128)S(1)}, f32[2,8,128]{2,1,0:T(8,128)S(1)}) conditional(s32[]{:T(128)} %convert_element_type.33, () %tuple.32, (pred[128,512]{1,0:T(8,128)(4,1)S(1)}, bf16[512,256]{1,0:T(8,128)(2,1)S(1)}, bf16[2,8,128,128]{2,3,1,0:T(8,128)(2,1)S(1)}, ...), branch_computations={%region_2.3_spmd, %region_3.6_spmd} | conditional | flops 1889804288 | bytes 16023584 | solution.py:95
  46.5 1.0 select_reduce_fusion
  48.1 2.0 %fusion.1 = f32[2,8,128]{2,1,0:T(8,128)S(1)} fusion(f32[2,8,128,512]{3,2,1,0:T(8,128)S(1)} %get-tuple-element.97, f32[2,8,128]{2,1,0:T(8,128)} %get-tuple-element.106, pred[128,512]{1,0:T(8,128)(4,1)S(1)} %get-tuple-element.55), kind=kLoop, calls=%fused_computation.3 | loop fusion | flops 4192256 | bytes 4276224 | tf_op jit(solution)/shard_map/cond/branch_1_fun/reduce_sum | solution.py:91
  50.0 3.5 %fusion.6 = f32[2,8,128,128]{3,2,1,0:T(8,128)S(1)} fusion(f32[2,8,128,512]{3,2,1,0:T(8,128)S(1)} %get-tuple-element.97, f32[2,8,128]{2,1,0:T(8,128)} %get-tuple-element.106, pred[128,512]{1,0:T(8,128)(4,1)S(1)} %get-tuple-element.55, f32[2,8,128]{2,1,0:T(8,128)S(1)} %get-tuple-element.94, bf16[512,2,128,1]{2,1,0,3:T(2,128)(2,1)S(1)} %bitcast.59), kind=kOutput, calls=%fused_computation.8 | convolution fusion | flops 1614020608 | bytes 5586944 | tf_op jit(solution)/shard_map/cond/branch_1_fun/kgtr,rkd->kgtd/dot_general | solution.py:86
  53.5 0.7 fusion.27
  54.3 8.6 %conditional.3 = (f32[2,8,128,128]{3,2,1,0:T(8,128)}, f32[512,2,256]{0,2,1:T(8,128)}) conditional(s32[]{:T(128)} %convert_element_type.33, () %tuple.31, (pred[128,512]{1,0:T(8,128)(4,1)S(1)}, bf16[512,256]{1,0:T(8,128)(2,1)S(1)}, bf16[2,8,128,128]{2,3,1,0:T(8,128)(2,1)S(1)}, f32[2,8,128]{2,1,0:T(8,128)}, f32[2,8,128]{2,1,0:T(8,128)S(1)}, ...), branch_computations={%region_6.7_spmd, %region_7.9_spmd} | conditional | flops 1353842688 | bytes 31391788 | solution.py:143
  54.3 0.7 add.60
  55.8 0.8 fusion.21
  56.7 1.1 %fusion.14 = f32[2,512,128,1]{1,2,3,0:T(8,128)S(1)} fusion(bf16[2,8,128,128]{2,3,1,0:T(8,128)(2,1)S(1)} %copy-done.2, f32[2,8,128,512]{3,2,1,0:T(8,128)S(1)} %fusion.21, f32[2,8,128]{2,1,0:T(8,128)S(1)} %add.60, pred[128,512]{1,0:T(8,128)(4,1)S(1)} %get-tuple-element.59), kind=kOutput, calls=%fused_computation.20 | convolution fusion | flops 272629760 | bytes 5316608 | tf_op jit(solution)/shard_map/cond/branch_1_fun/kgtr,kgtd->rkd/dot_general | solution.py:125
  57.8 1.8 %multiply_convert_fusion = bf16[2,8,128,512]{3,2,1,0:T(8,128)(2,1)S(1)} fusion(f32[2,8,128,512]{3,2,1,0:T(8,128)S(1)} %fusion.21, bf16[2,8,128,128]{2,3,1,0:T(8,128)(2,1)S(1)} %copy-done.2, f32[2,8,128]{2,1,0:T(8,128)S(1)} %multiply_reduce_fusion, f32[2,8,128]{2,1,0:T(8,128)S(1)} %add.60, pred[128,512]{1,0:T(8,128)(4,1)S(1)} %get-tuple-element.59, ...), kind=kOutput, calls=%fused_computation.17 | convolution fusion | flops 274726912 | bytes 7159808 | tf_op jit(solution)/shard_map/cond/branch_1_fun/kgtd,rkd->kgtr/dot_general | solution.py:109
  60.1 1.7 %fusion.19 = f32[2,8,128,128]{3,2,1,0:T(8,128)} fusion(bf16[2,8,128,512]{3,2,1,0:T(8,128)(2,1)S(1)} %multiply_convert_fusion, bf16[512,2,128,1]{2,1,0,3:T(2,128)(2,1)S(1)} %bitcast.51), kind=kOutput, calls=%fused_computation.27 | convolution fusion | flops 268435456 | bytes 3407872 | tf_op jit(solution)/shard_map/cond/branch_1_fun/kgtr,rkd->kgtd/dot_general | solution.py:113
  61.8 1.1 %pad_maximum_fusion = f32[512,2,256]{0,2,1:T(8,128)} fusion(f32[512,1,256]{0,2,1:T(8,128)S(1)} %bitcast.58, f32[512,1,256]{0,2,1:T(8,128)S(1)} %bitcast.55), kind=kLoop, calls=%fused_computation.24 | loop fusion | flops 262144 | bytes 2097152 | tf_op jit(solution)/shard_map/cond/branch_1_fun/stack | solution.py:131
  62.9 2.5 %copy.34 = f32[512,2,256]{2,0,1:T(8,128)} copy(f32[512,2,256]{0,2,1:T(8,128)} %get-tuple-element.83) | data formatting | bytes 2097152 | tf_op jit(solution)/shard_map/cond | solution.py:143
  65.5 1.4 %fusion.25 = bf16[128,2,8,128]{3,0,2,1:T(8,128)(2,1)S(1)} fusion(f32[2,8,128,128]{3,2,1,0:T(8,128)} %get-tuple-element.82), kind=kLoop, calls=%fused_computation.34 | loop fusion | flops 524288 | bytes 1572864 | tf_op jit(solution)/shard_map/convert_element_type | solution.py:179
  67.2 0.9 copy.69
  68.1 25.6 %reduce-scatter.2.cloned.1.call-done = f32[128,2,256]{2,0,1:T(8,128)} async-done(((f32[512,2,256]{2,0,1:T(8,128)}), f32[128,2,256]{2,0,1:T(8,128)}) %reduce-scatter.2.cloned.1.call-update) | async-done | bytes 262160 | tf_op jit(solution)/shard_map/reduce_scatter | solution.py:174
  93.7 1.0 convert.4
  (25 shorter events, 4.8 us)
Async XLA Ops:
  7.2 2.6 %copy-start = (s32[4,2]{0,1:T(2,128)S(1)}, s32[4,2]{0,1:T(2,128)}, u32[]{:S(2)}) copy-start(s32[4,2]{0,1:T(2,128)} %param.15) | copy-start | bytes 100
  7.2 86.5 %reduce-scatter.2.cloned.1.call-start = ((), (), s32[]{:S(2)}) async-start(), calls=%async_computation.1 | async-start | bytes 1310720 | tf_op jit(solution)/shard_map/reduce_scatter | solution.py:174
  45.0 0.8 copy-start.1
  55.7 1.0 %copy-start.2 = (bf16[2,8,128,128]{2,3,1,0:T(8,128)(2,1)S(1)}, bf16[2,8,128,128]{2,3,1,0:T(8,128)(2,1)}, u32[]{:S(2)}) copy-start(bf16[2,8,128,128]{2,3,1,0:T(8,128)(2,1)} %get-tuple-element.64) | copy-start | bytes 1572868 | tf_op jit(solution)/shard_map/cond
Sparse Core Ops, SparseCore 0:
  65.6 28.0 reduce-scatter.1
where the time goes:
time: 103 us; the launch traced here: 102 us
  blocking collectives  30.7 us (30%)
  waiting for transfers between devices  25.6 us (25%)
  between operations  15.4 us (15%)
  matrix products  10.3 us (10%)
  local copies, waits for them, and re-layouts  10.2 us (10%)
  other arithmetic  9.81 us (10%)
    reduce_scatter x1, waiting for transfers between devices, on_device(): summed = lax.psum_scatter(key_grads, 'ctx', scatter_dimension=0, tiled=True)  25.6 us
    all_gather x1, blocking collectives, on_device(): lax.all_gather(keys, 'ctx', axis=0, tiled=True)  15.8 us
    all_gather x1, blocking collectives, on_device(): lax.all_gather(values, 'ctx', axis=0, tiled=True)  14.8 us
    unnamed x7, local copies, waits for them, and re-layouts  4.36 us
    dot_general x1, matrix products, forward_update(): jnp.einsum('kgtr,rkd->kgtd', weights, value_heads, precision=lax.Precisio...  3.49 us
    cond x1, local copies, waits for them, and re-layouts, step(): return lax.cond(jnp.any(allowed), step_update, lambda state: state, carry)  2.55 us
  transfers between devices with their start and end apart: 1, of which 1 were waited for; matrix products, arithmetic and copies ran while one was open for 3% of the time, Pallas kernels for 0%

commit v1 on v0

--- a/solution.py
+++ b/solution.py
@@ -9,6 +9,27 @@
 HEAD_SIZE = 128
 BLOCK = 128
 NEG = -1e30
+
+
+def gather_around(x, axis, dim):
+    devices, place, extent = (lax.axis_size(axis), lax.axis_index(axis), x.shape[dim])
+    upward = [(i, (i + 1) % devices) for i in range(devices)]
+    left = [(i, (i - 1) % devices) for i in range(devices)]
+    result = jnp.zeros((*x.shape[:dim], devices * extent, *x.shape[dim + 1 :]), x.dtype)
+    result = lax.dynamic_update_slice_in_dim(result, x, place * extent, axis=dim)
+    from_left = from_right = x
+    half = devices // 2
+    for step in range(1, half + 1):
+        from_left = lax.ppermute(from_left, axis, upward)
+        result = lax.dynamic_update_slice_in_dim(
+            result, from_left, (place - step) % devices * extent, axis=dim
+        )
+        if step < devices - half:
+            from_right = lax.ppermute(from_right, axis, left)
+            result = lax.dynamic_update_slice_in_dim(
+                result, from_right, (place + step) % devices * extent, axis=dim
+            )
+    return result
 
 
 def heads_first(dense_matrix, key_value_count):
@@ -167,7 +188,7 @@
     query_grad, key_grads = sweep(
         both_step,
         (query_zero, grad_zero),
-        lax.all_gather(keys, "ctx", axis=0, tiled=True),
+        gather_around(keys, "ctx", 0),
         lax.all_gather(values, "ctx", axis=0, tiled=True),
         jnp.int32(0),
     )

time: 103 us -> 115 us (1.12)
  starting transfers between devices: 0.04 us -> 7.59 us
  local copies, waits for them, and re-layouts: 10.2 us -> 16.1 us
  other arithmetic: 9.81 us -> 11.8 us
  waiting for transfers between devices: 25.6 us -> 23.7 us
  blocking collectives: 30.7 us -> 29.2 us
    ppermute x0 -> x3, starting transfers between devices: none -> 7.55 us  [the longest x1 5.05 us: gather_around(): from_right = lax.ppermute(from_right, axis, left)]
    dynamic_update_slice x0 -> x4, local copies, waits for them, and re-layouts: none -> 2.62 us  [the longest x2 1.73 us: gather_around(): lax.dynamic_update_slice_in_dim(result, from_left, (place - step) % devic...]
    reduce_scatter x1, waiting for transfers between devices: 25.6 us -> 23.7 us  [on_device(): summed = lax.psum_scatter(key_grads, 'ctx', scatter_dimension=0, tiled=True)]
    unnamed x7 -> x10, local copies, waits for them, and re-layouts: 4.36 us -> 5.18 us
  transfers between devices with their start and end apart: 1 -> 4, of which waited for: 1 -> 1; matrix products, arithmetic and copies ran while one was open for 3% -> 18% of each run, Pallas kernels for 0% -> 0%
where the time goes in v1:
time: 115 us; the launch traced here: 114 us
  blocking collectives  29.2 us (25%)
  waiting for transfers between devices  23.7 us (21%)
  local copies, waits for them, and re-layouts  16.1 us (14%)
  between operations  15.4 us (13%)
  other arithmetic  11.8 us (10%)
  matrix products  10.4 us (9%)
  starting transfers between devices  7.59 us (7%)
    reduce_scatter x1, waiting for transfers between devices, on_device(): summed = lax.psum_scatter(key_grads, 'ctx', scatter_dimension=0, tiled=True)  23.7 us
    all_gather x1, blocking collectives, on_device(): lax.all_gather(keys, 'ctx', axis=0, tiled=True)  14.8 us
    all_gather x1, blocking collectives, on_device(): lax.all_gather(values, 'ctx', axis=0, tiled=True)  14.4 us
    unnamed x10, local copies, waits for them, and re-layouts  5.18 us
    ppermute x1, starting transfers between devices, gather_around(): from_right = lax.ppermute(from_right, axis, left)  5.05 us
    dot_general x1, matrix products, forward_update(): jnp.einsum('kgtr,rkd->kgtd', weights, value_heads, precision=lax.Precisio...  3.49 us
    cond x1, local copies, waits for them, and re-layouts, step(): return lax.cond(jnp.any(allowed), step_update, lambda state: state, carry)  2.55 us
    ppermute x2, starting transfers between devices, gather_around(): from_left = lax.ppermute(from_left, axis, upward)  2.5 us
  transfers between devices with their start and end apart: 4, of which 1 were waited for; matrix products, arithmetic and copies ran while one was open for 18% of the time, Pallas kernels for 0%

profile of v1, /device:TPU:0, one launch (start us, length us, event | category | flops | bytes accessed | tf_op | source)
XLA Modules:
  0.0 114.4 jit_solution(18164148165246017067)
XLA Ops:
  7.2 1.6 %copy.57 = bf16[128,256]{0,1:T(8,128)(2,1)} copy(bf16[128,256]{1,0:T(8,128)(2,1)} %param.11) | data formatting | bytes 131072 | tf_op args[1]
  8.8 5.0 %collective-permute-start.1 = (bf16[128,256]{0,1:T(8,128)(2,1)}, bf16[128,256]{0,1:T(8,128)(2,1)}, u32[]{:S(2)}, u32[]{:S(2)}) collective-permute-start(bf16[128,256]{0,1:T(8,128)(2,1)} %copy.57), channel_id=1, source_target_pairs={{0,12},{4,0},{8,4},{12,8},{1,13},{5,1},{9,5},{13,9},{2,14},{6,2},{... | collective-permute-start | bytes 196616 | tf_op jit(solution)/shard_map/ppermute | solution.py:28
  14.6 1.2 %dynamic_slice.12 = s32[1]{0:T(128)} dynamic-slice(s32[4]{0:T(128)} %param.14, s32[]{:T(128)S(6)} %select_n.76), dynamic_slice_sizes={1} | dynamic-slice | bytes 12 | tf_op jit(solution)/shard_map/dynamic_slice | solution.py:80
  18.3 1.3 %copy.59 = bf16[128,2048]{0,1:T(8,128)(2,1)S(1)} copy(bf16[128,2048]{1,0:T(8,128)(2,1)} %param.10) | data formatting | bytes 1048576 | tf_op args[0]
  19.6 1.3 %copy.62 = bf16[128,2048]{0,1:T(8,128)(2,1)S(1)} copy(bf16[128,2048]{1,0:T(8,128)(2,1)} %param.13) | data formatting | bytes 1048576 | tf_op args[3]
  22.2 14.8 %all_gather.7 = bf16[512,256]{1,0:T(8,128)(2,1)} all-gather(bf16[128,256]{1,0:T(8,128)(2,1)S(1)} %copy-done.1), channel_id=1, replica_groups=mesh['grp'=2,'ctx'=4,'head'=4] {'ctx'}, dimensions={0}, use_global_device_ids=true | all-gather | bytes 327680 | tf_op jit(solution)/shard_map/all_gather | solution.py:177
  37.0 2.5 %collective-permute-start.2 = (bf16[128,256]{0,1:T(8,128)(2,1)}, bf16[128,256]{0,1:T(8,128)(2,1)}, u32[]{:S(2)}, u32[]{:S(2)}) collective-permute-start(bf16[128,256]{0,1:T(8,128)(2,1)} %collective-permute-done), channel_id=1, source_target_pairs={{0,4},{4,8},{8,12},{12,0},{1,5},{5,9},{9,13},{13,1},{2,6},{6,10},{... | collective-permute-start | bytes 196616 | tf_op jit(solution)/shard_map/ppermute | solution.py:23
  39.5 14.4 %all_gather.8 = bf16[512,256]{1,0:T(8,128)(2,1)S(1)} all-gather(bf16[128,256]{1,0:T(8,128)(2,1)S(1)} %copy-done.4), channel_id=1, replica_groups=mesh['grp'=2,'ctx'=4,'head'=4] {'ctx'}, dimensions={0}, use_global_device_ids=true | all-gather | bytes 327680 | tf_op jit(solution)/shard_map/all_gather | solution.py:192
  53.9 11.2 %conditional.2 = (f32[2,8,128]{2,1,0:T(8,128)}, f32[2,8,128]{2,1,0:T(8,128)S(1)}, f32[2,8,128,128]{3,2,1,0:T(8,128)S(1)}, f32[2,8,128]{2,1,0:T(8,128)}) conditional(s32[]{:T(128)} %convert_element_type.37, () %tuple.78, (pred[128,512]{0,1:T(8,128)(4,1)}, bf16[512,256]{1,0:T(8,128)(2,1)}, bf16[2,8,128,128]{2,3,1,0:T(8,128)(2,1)S(1)}, ...), branch_computations={%region_2.3_spmd, %region_3.6_spmd} | conditional | flops 1889804288 | bytes 17203260 | solution.py:116
  54.7 1.0 copy.60
  55.7 1.0 reshape.146
  56.7 1.0 select_reduce_fusion
  58.3 2.0 %fusion.1 = f32[2,8,128]{2,1,0:T(8,128)S(1)} fusion(f32[2,8,128,512]{3,2,1,0:T(8,128)S(1)} %get-tuple-element.545, f32[2,8,128]{2,1,0:T(8,128)} %get-tuple-element.554, pred[128,512]{1,0:T(8,128)(4,1)S(1)} %copy.60), kind=kLoop, calls=%fused_computation.3 | loop fusion | flops 4192256 | bytes 4276224 | tf_op jit(solution)/shard_map/cond/branch_1_fun/reduce_sum | solution.py:112
  60.3 3.5 %fusion.6 = f32[2,8,128,128]{3,2,1,0:T(8,128)S(1)} fusion(f32[2,8,128,512]{3,2,1,0:T(8,128)S(1)} %get-tuple-element.545, f32[2,8,128]{2,1,0:T(8,128)} %get-tuple-element.554, pred[128,512]{1,0:T(8,128)(4,1)S(1)} %copy.60, f32[2,8,128]{2,1,0:T(8,128)S(1)} %get-tuple-element.542, bf16[512,2,128,1]{2,1,0,3:T(2,128)(2,1)S(1)} %bitcast.79), kind=kOutput, calls=%fused_computation.8 | convolution fusion | flops 1614020608 | bytes 5586944 | tf_op jit(solution)/shard_map/cond/branch_1_fun/kgtr,rkd->kgtd/dot_general | solution.py:107
  63.8 1.3 %fusion.23 = (f32[2,8,128]{2,1,0:T(8,128)}, f32[2,8,128]{2,1,0:T(8,128)S(1)}) fusion(f32[2,8,128]{2,1,0:T(8,128)S(1)} %fusion.1, f32[2,8,128]{2,1,0:T(8,128)} %get-tuple-element.554), kind=kLoop, calls=%fused_computation.47 | loop fusion | flops 6144 | bytes 32768 | tf_op jit(solution)/shard_map/log | solution.py:183
  65.1 11.9 %conditional.3 = (f32[2,8,128,128]{3,2,1,0:T(8,128)}, f32[512,2,256]{0,2,1:T(8,128)}) conditional(s32[]{:T(128)} %convert_element_type.37, () %tuple.77, (pred[128,512]{0,1:T(8,128)(4,1)}, s32[]{:T(128)}, bf16[128,256]{1,0:T(8,128)(2,1)S(1)}, s32[]{:T(128)}, bf16[128,256]{0,1:T(8,128)(2,1)}, /*index=5*/s32[]{:T(128)}, ...), branch_computations={%region_6.7_spmd, %region_7.9_spmd.clone.clone} | conditional | flops 1353842688 | bytes 29983356 | solution.py:164
  65.2 1.2 %multiply_reduce_fusion = f32[2,8,128]{2,1,0:T(8,128)} fusion(f32[2,8,128,128]{3,2,1,0:T(8,128)S(1)} %get-tuple-element.517, f32[2,8,128,128]{3,2,1,0:T(8,128)S(1)} %get-tuple-element.516, f32[2,8,128]{2,1,0:T(8,128)S(1)} %get-tuple-element.515), kind=kLoop, calls=%fused_computation.25 | loop fusion | flops 784384 | bytes 2113536 | tf_op jit(solution)/shard_map/reduce_sum | solution.py:184
  70.8 1.0 fusion.14
  71.8 1.4 %multiply_convert_fusion = bf16[2,8,128,512]{2,3,1,0:T(8,128)(2,1)S(1)} fusion(f32[2,512,8,128]{3,1,2,0:T(8,128)S(1)} %fusion.25, bf16[2,8,128,128]{2,3,1,0:T(8,128)(2,1)S(1)} %get-tuple-element.514, f32[2,8,128]{2,1,0:T(8,128)S(1)} %copy-done.5, f32[2,8,128]{2,1,0:T(8,128)S(1)} %add.148, pred[128,512]{0,1:T(8,128)(4,1)S(1)} %copy-done.3, ...), kind=kOutput, calls=%fused_computation.18 | convolution fusion | flops 274726912 | bytes 7159808 | tf_op jit(solution)/shard_map/cond/branch_1_fun/kgtd,rkd->kgtr/dot_general | solution.py:130
  74.0 2.0 %fusion.26 = f32[2,8,128,128]{3,2,1,0:T(8,128)} fusion(bf16[2,8,128,512]{2,3,1,0:T(8,128)(2,1)S(1)} %multiply_convert_fusion, bf16[512,2,128,1]{0,2,3,1:T(8,128)(2,1)S(1)} %bitcast.70), kind=kOutput, calls=%fused_computation.49 | convolution fusion | flops 268435456 | bytes 3407872 | tf_op jit(solution)/shard_map/cond/branch_1_fun/kgtr,rkd->kgtd/dot_general | solution.py:134
  75.9 1.1 pad_maximum_fusion
  77.0 2.5 %copy.66 = f32[512,2,256]{2,0,1:T(8,128)} copy(f32[512,2,256]{0,2,1:T(8,128)} %get-tuple-element.393) | data formatting | bytes 2097152 | tf_op jit(solution)/shard_map/cond | solution.py:164
  79.6 1.4 %fusion.21 = bf16[128,2,8,128]{3,0,2,1:T(8,128)(2,1)S(1)} fusion(f32[2,8,128,128]{3,2,1,0:T(8,128)} %get-tuple-element.392), kind=kLoop, calls=%fused_computation.34 | loop fusion | flops 524288 | bytes 1572864 | tf_op jit(solution)/shard_map/convert_element_type | solution.py:200
  82.2 23.7 %reduce-scatter.2.cloned.1.call-done = f32[128,2,256]{2,0,1:T(8,128)} async-done(((f32[512,2,256]{2,0,1:T(8,128)}), f32[128,2,256]{2,0,1:T(8,128)}) %reduce-scatter.2.cloned.1.call-update) | async-done | bytes 262160 | tf_op jit(solution)/shard_map/reduce_scatter | solution.py:195
  (44 shorter events, 12.6 us)
Async XLA Ops:
  7.2 9.3 %copy-start = (s32[4,2]{0,1:T(2,128)S(1)}, s32[4,2]{0,1:T(2,128)}, u32[]{:S(2)}) copy-start(s32[4,2]{0,1:T(2,128)} %param.15) | copy-start | bytes 100
  7.2 15.0 %copy-start.1 = (bf16[128,256]{1,0:T(8,128)(2,1)S(1)}, bf16[128,256]{1,0:T(8,128)(2,1)}, u32[]{:S(2)}) copy-start(bf16[128,256]{1,0:T(8,128)(2,1)} %param.11) | copy-start | bytes 196612
  7.2 32.3 %copy-start.4 = (bf16[128,256]{1,0:T(8,128)(2,1)S(1)}, bf16[128,256]{1,0:T(8,128)(2,1)}, u32[]{:S(2)}) copy-start(bf16[128,256]{1,0:T(8,128)(2,1)} %param.12) | copy-start | bytes 196612
  7.2 98.7 %reduce-scatter.2.cloned.1.call-start = ((), (), s32[]{:S(2)}) async-start(), calls=%async_computation.1 | async-start | bytes 1310720 | tf_op jit(solution)/shard_map/reduce_scatter | solution.py:195
  8.8 56.3 %collective-permute-start.1 = (bf16[128,256]{0,1:T(8,128)(2,1)}, bf16[128,256]{0,1:T(8,128)(2,1)}, u32[]{:S(2)}, u32[]{:S(2)}) collective-permute-start(bf16[128,256]{0,1:T(8,128)(2,1)} %copy.57), channel_id=1, source_target_pairs={{0,12},{4,0},{8,4},{12,8},{1,13},{5,1},{9,5},{13,9},{2,14},{6,2},{... | collective-permute-start | bytes 196616 | tf_op jit(solution)/shard_map/ppermute | solution.py:28
  13.9 23.1 %collective-permute-start = (bf16[128,256]{0,1:T(8,128)(2,1)}, bf16[128,256]{0,1:T(8,128)(2,1)}, u32[]{:S(2)}, u32[]{:S(2)}) collective-permute-start(bf16[128,256]{0,1:T(8,128)(2,1)} %copy.57), channel_id=1, source_target_pairs={{0,4},{4,8},{8,12},{12,0},{1,5},{5,9},{9,13},{13,1},{2,6},{6,10},{... | collective-permute-start | bytes 196616 | tf_op jit(solution)/shard_map/ppermute | solution.py:23
  37.0 28.1 %collective-permute-start.2 = (bf16[128,256]{0,1:T(8,128)(2,1)}, bf16[128,256]{0,1:T(8,128)(2,1)}, u32[]{:S(2)}, u32[]{:S(2)}) collective-permute-start(bf16[128,256]{0,1:T(8,128)(2,1)} %collective-permute-done), channel_id=1, source_target_pairs={{0,4},{4,8},{8,12},{12,0},{1,5},{5,9},{9,13},{13,1},{2,6},{6,10},{... | collective-permute-start | bytes 196616 | tf_op jit(solution)/shard_map/ppermute | solution.py:23
  56.7 3.6 %copy-start.2 = (bf16[512,2,128]{2,1,0:T(2,128)(2,1)S(1)}, bf16[512,2,128]{2,1,0:T(2,128)(2,1)}, u32[]{:S(2)}) copy-start(bf16[512,2,128]{2,1,0:T(2,128)(2,1)} %reshape.147) | copy-start | bytes 786436 | tf_op jit(solution)/shard_map/cond
  65.2 5.6 %copy-start.3 = (pred[128,512]{0,1:T(8,128)(4,1)S(1)}, pred[128,512]{0,1:T(8,128)(4,1)}, u32[]{:S(2)}) copy-start(pred[128,512]{0,1:T(8,128)(4,1)} %get-tuple-element.504) | copy-start | bytes 196612 | tf_op jit(solution)/shard_map/cond
  70.8 1.0 copy-start.5
Sparse Core Ops, SparseCore 0:
  79.7 26.1 reduce-scatter.1
